TPU v7x, 32 devices: a whole 2x2x4 slice. The times are simulated.
32 devices in a mesh: cg: 8 (over z, x), vg: 4 (over y, core).
Axes of the slice: x: 2, y: 2, z: 4, core: 2. Of those that a mesh axis runs over, the one named last changes fastest.
Arguments:
- con_embed: float32 [32768, 128], P(('cg', 'vg')), may hold values from -6 to 6
- var_embed: float32 [32768, 128], P(('vg', 'cg')), may hold values from -6 to 6
- row_coef: float32 [32768], P(('cg', 'vg')), may hold values from 0.3 to 3
- col_coef: float32 [32768], P(('vg', 'cg')), may hold values from 0.3 to 3
- self_weight: float32 [128, 128], replicated, may hold values from -0.5 to 0.5
- msg_weight: float32 [128, 128], replicated, may hold values from -0.0234375 to 0.0234375
- timestep: int32 [1], replicated, may hold values from 0 to 999
- tile_rows: int32 [8, 4, 16], P('cg', 'vg'), may hold values from 0 to 7, as said below
- tile_cols: int32 [8, 4, 16], P('cg', 'vg'), may hold values from 0 to 15, as said below
- pattern: bfloat16 [8, 4, 16, 512, 512], P('cg', 'vg'), may hold values from -6 to 6
- cotangent: float32 [32768, 128], P(('cg', 'vg')), may hold values from -6 to 6
Outputs:
- con_update: float32 [32768, 128], P(('cg', 'vg'))
- grad_con: float32 [32768, 128], P(('cg', 'vg'))
- grad_var: float32 [32768, 128], P(('vg', 'cg'))
- grad_msg: float32 [128, 128], replicated
- grad_self: float32 [128, 128], replicated
Inputs may be any that keep to these rules, and one draw needn't show every extreme that they name: `tile_rows`: every device lists tile row 0 and tile row 7; a device lists distinct tiles unless 16 exceeds 8 * 16, and repeated tiles add. `tile_cols`: every device lists tile column 0 and tile column 15, together with the rows above: tiles (0, 0) and (7, 15) are on every list.
All inputs are finite; a program needn't handle non-finite values.
Results may differ from a plain program's by a relative error of at most 0.007.
Values may be sent and summed in bfloat16 or wider, within the bound.
A program may use at most 128 MiB of HBM per device.

v0:
```python
import functools
import math

import jax
import jax.numpy as jnp
from jax import lax
from jax.experimental import pallas as pl
from jax.experimental.pallas import tpu as pltpu
from jax.sharding import PartitionSpec as P

H = 128
TB = 512
CHUNKS = 4
MESH = pl.DeviceIdType.MESH
HIGHEST = lax.Precision.HIGHEST
F32 = jnp.float32
BF16 = jnp.bfloat16


def rcopy(src, dst, send_sem, recv_sem, device):
    return pltpu.make_async_remote_copy(
        src_ref=src, dst_ref=dst, send_sem=send_sem, recv_sem=recv_sem,
        device_id=device, device_id_type=MESH,
    )


def rows(index, size):
    return pl.ds(pl.multiple_of(index * size, size), size)


def dot(a, b, dims=((1,), (0,))):
    return lax.dot_general(a, b, (dims, ((), ())), precision=HIGHEST, preferred_element_type=F32)


def column(coef_ref, out_ref):
    for i in range(coef_ref.shape[0]):
        out_ref[pl.ds(i * H, H), :] = jnp.broadcast_to(coef_ref[pl.ds(i, 1), :], (H, H)).T


class Total:
    def __init__(self, n_cg, n_vg, local, out, cuts, quarters, sem):
        self.n_cg, self.n_vg = n_cg, n_vg
        self.local, self.out, self.cuts, self.quarters, self.sem = local, out, cuts, quarters, sem
        self.cg, self.vg = lax.axis_index("cg"), lax.axis_index("vg")
        self.size = H // n_vg

    def a(self, j):
        v = lax.rem(self.vg + j, self.n_vg)
        return rcopy(
            self.local.at[rows(v, self.size), :], self.cuts.at[j - 1],
            self.sem.at[0, j], self.sem.at[1, j], (self.cg, v),
        )

    def b(self, j):
        c = lax.rem(self.cg + j, self.n_cg)
        block = self.quarters.at[self.cg]
        return rcopy(block, block, self.sem.at[2, j], self.sem.at[3, j], (c, self.vg))

    def b_wait(self, j):
        c = lax.rem(self.cg + self.n_cg - j, self.n_cg)
        block = self.quarters.at[c]
        rcopy(block, block, self.sem.at[2, j], self.sem.at[3, j], (c, self.vg)).wait_recv()

    def c(self, j):
        v = lax.rem(self.vg + j, self.n_vg)
        block = self.out.at[rows(self.vg, self.size), :]
        return rcopy(block, block, self.sem.at[4, j], self.sem.at[5, j], (self.cg, v))

    def c_wait(self, j):
        v = lax.rem(self.vg + self.n_vg - j, self.n_vg)
        block = self.out.at[rows(v, self.size), :]
        rcopy(block, block, self.sem.at[4, j], self.sem.at[5, j], (self.cg, v)).wait_recv()

    def start(self):
        for j in range(1, self.n_vg):
            self.a(j).start()

    def second(self):
        value = self.local[rows(self.vg, self.size), :]
        for j in range(1, self.n_vg):
            self.a(j).wait_recv()
            value = value + self.cuts[j - 1]
        self.quarters[self.cg] = value
        for j in range(1, self.n_cg):
            self.b(j).start()

    def third(self):
        for j in range(1, self.n_cg):
            self.b_wait(j)
            self.b(j).wait_send()
        value = self.quarters[0]
        for c in range(1, self.n_cg):
            value = value + self.quarters[c]
        self.out[rows(self.vg, self.size), :] = value
        for j in range(1, self.n_vg):
            self.c(j).start()

    def finish(self):
        for j in range(1, self.n_vg):
            self.c_wait(j)
            self.c(j).wait_send()
            self.a(j).wait_send()


def layer_kernel(
    n_cg, n_vg, row_ref, col_ref, chain_ref, pattern_hbm, var_ref, msg_w_ref, col_coef_ref, con_hbm, cot_hbm,
    self_w_ref, row_coef_ref, time_ref,
    update_ref, grad_con_ref, grad_var_ref, grad_msg_ref, grad_self_ref,
    pattern, con_ref, cot_ref, coef, pre, projected, whole, acc,
    to_core, from_core, to_peer, from_peer, to_x, from_x, to_z, from_z, local_msg, local_self,
    cuts_a, cuts_b, quarters_a, quarters_b,
    load_sem, gz_send, gx_send, gz_recv, gx_recv,
    core_send, core_recv, peer_send, peer_recv, own_send, pass_send, block_recv, pair_recv,
    x_send, x_recv, z_send, z_recv, sem_a, sem_b,
):
    n_z, n_hi = n_cg // 2, n_vg // 2
    cg, vg = lax.axis_index("cg"), lax.axis_index("vg")
    z, x = cg // 2, cg % 2
    hi, core = vg // 2, vg % 2
    count = pattern.shape[0]
    size = var_ref.shape[0]
    piece = size // CHUNKS
    chunks = range(CHUNKS)
    x_peer, pair = (z * 2 + 1 - x, vg), (cg, hi * 2 + 1 - core)

    barrier = pltpu.get_barrier_semaphore()
    for j in range(1, n_cg):
        pl.semaphore_signal(barrier, inc=1, device_id=(lax.rem(cg + j, n_cg), vg), device_id_type=MESH)
    for j in range(1, n_vg):
        pl.semaphore_signal(barrier, inc=1, device_id=(cg, lax.rem(vg + j, n_vg)), device_id_type=MESH)
    loads = [
        pltpu.make_async_copy(con_hbm, con_ref, load_sem.at[0]),
        pltpu.make_async_copy(cot_hbm, cot_ref, load_sem.at[1]),
        pltpu.make_async_copy(pattern_hbm, pattern, load_sem.at[2]),
    ]
    for load in loads:
        load.start()

    def cut(block, k):
        return rows(block * CHUNKS + k, piece)

    def here(k):
        return pl.ds(k * piece, piece)

    def spot(block, k):
        return block * (size // TB) + (k * piece) // TB, pl.ds((k * piece) % TB, piece)

    def gz_copy(zs, way, k):
        block = projected.at[spot(zs * 2 + x, k)]
        step = 1 if way == 0 else -1
        return rcopy(block, block, gz_send.at[way, zs, k], gz_recv.at[zs, k], ((z + step) * 2 + x, vg))

    def gx_copy(zs, k):
        block = projected.at[spot(zs * 2 + x, k)]
        return rcopy(block, block, gx_send.at[zs, k], gx_recv.at[zs, k], x_peer)

    def gx_wait(zs, k):
        block = projected.at[spot(zs * 2 + 1 - x, k)]
        rcopy(block, block, gx_send.at[zs, k], gx_recv.at[zs, k], x_peer).wait_recv()

    def on(zs, way, act):
        if way == 0:
            pl.when((zs >= 0) & (zs <= z) & (z + 1 < n_z))(act)
        else:
            pl.when((zs < n_z) & (zs >= z) & (z >= 1))(act)

    column(col_coef_ref, coef)
    for k in chunks:
        projected[spot(cg, k)] = (dot(var_ref[here(k), :], msg_w_ref[...]) * coef[here(k), :]).astype(BF16)
        if k == 0:
            pl.semaphore_wait(barrier, n_cg + n_vg - 2)
        for way in (0, 1):
            on(z, way, lambda way=way: gz_copy(z, way, k).start())
        gx_copy(z, k).start()

    acc[count] = jnp.zeros(acc.shape[1:], F32)

    for d in range(1, n_z):
        for k in chunks:
            for way in (0, 1):
                zs = z - d if way == 0 else z + d

                @pl.when((zs >= 0) & (zs < n_z))
                def _(zs=zs, way=way, k=k):
                    gz_copy(zs, way, k).wait_recv()
                    on(zs, way, lambda: gz_copy(zs, way, k).start())
                    gx_copy(zs, k).start()

    for load in loads[:2]:
        load.wait()
    pre[...] = dot(con_ref[...], self_w_ref[...]) + time_ref[...]
    loads[2].wait()
    for k in chunks:
        for zs in range(n_z):
            gx_wait(zs, k)

    row_blocks = whole.shape[0]
    last_f, prev_b, last_b = count, count + row_blocks, 2 * count + row_blocks

    def tile_step(prev, from_ref, source_ref, dims):
        def step(k, carry):
            source = source_ref[from_ref[k]]
            product = lax.dot_general(pattern[k], source, (dims, ((), ())), preferred_element_type=F32)
            acc[k] = product + acc[chain_ref[prev + k]]
            return carry

        lax.fori_loop(0, count, step, 0, unroll=4)

    def part(last, block, k):
        tile = chain_ref[last + block * (size // TB) + (k * piece) // TB]
        return acc[tile, pl.ds((k * piece) % TB, piece), :]

    tile_step(0, col_ref, projected, ((1,), (0,)))

    ups = [lax.rem(hi + j, n_hi) for j in range(n_hi)]
    downs = [lax.rem(hi + n_hi - j, n_hi) for j in range(n_hi)]

    def core_copy(h, k):
        return rcopy(
            to_core.at[cut(h, k), :], from_core.at[cut(h, k), :], core_send.at[h, k], core_recv.at[h, k], pair
        )

    def peer_copy(j, k):
        return rcopy(
            to_peer.at[cut(j - 1, k), :], from_peer.at[cut(j - 1, k), :],
            peer_send.at[j - 1, k], peer_recv.at[j - 1, k], (cg, ups[j] * 2 + core),
        )

    def own_copy(j, k):
        block = whole.at[spot(vg, k)]
        return rcopy(block, block, own_send.at[j - 1, k], block_recv.at[j - 1, k], (cg, ups[j] * 2 + core))

    def block_wait(j, k):
        block = whole.at[spot(downs[j] * 2 + core, k)]
        rcopy(block, block, own_send.at[j - 1, k], block_recv.at[j - 1, k], pair).wait_recv()

    def pass_copy(h, k):
        block = whole.at[spot(h * 2 + core, k)]
        return rcopy(block, block, pass_send.at[h, k], pair_recv.at[h, k], pair)

    def pass_wait(h, k):
        block = whole.at[spot(h * 2 + 1 - core, k)]
        rcopy(block, block, pass_send.at[h, k], pair_recv.at[h, k], pair).wait_recv()

    for j in list(range(1, n_hi)) + [0]:
        for k in chunks:
            to_core[cut(ups[j], k), :] = part(last_f, ups[j] * 2 + 1 - core, k).astype(BF16)
            core_copy(ups[j], k).start()
    for j in range(1, n_hi):
        for k in chunks:
            core_copy(ups[j], k).wait_recv()
            to_peer[cut(j - 1, k), :] = (
                part(last_f, ups[j] * 2 + core, k) + from_core[cut(ups[j], k), :].astype(F32)
            ).astype(BF16)
            peer_copy(j, k).start()
    column(row_coef_ref, coef)
    for k in chunks:
        core_copy(hi, k).wait_recv()
        messages = part(last_f, vg, k) + from_core[cut(hi, k), :].astype(F32)
        for j in range(1, n_hi):
            peer_copy(j, k).wait_recv()
            messages = messages + from_peer[cut(j - 1, k), :].astype(F32)
        preact = pre[here(k), :] + coef[here(k), :] * messages
        sig = jax.nn.sigmoid(preact)
        grad_pre = cot_ref[here(k), :] * sig * (1.0 + preact * (1.0 - sig))
        whole[spot(vg, k)] = (coef[here(k), :] * grad_pre).astype(BF16)
        for j in range(1, n_hi):
            own_copy(j, k).start()
        pass_copy(hi, k).start()
        update_ref[here(k), :] = con_ref[here(k), :] + preact * sig
        pre[here(k), :] = grad_pre
    local_self[...] = dot(con_ref[...], pre[...], ((0,), (0,)))
    small = Total(n_cg, n_vg, local_self, grad_self_ref, cuts_a, quarters_a, sem_a)
    small.start()
    grad_con_ref[...] = cot_ref[...] + dot(pre[...], self_w_ref[...], ((1,), (1,)))
    column(col_coef_ref, coef)
    for k in chunks:
        for j in range(1, n_hi):
            block_wait(j, k)
            pass_copy(downs[j], k).start()
    for h in range(n_hi):
        for k in chunks:
            pass_wait(h, k)

    tile_step(prev_b, row_ref, whole, ((0,), (0,)))

    def x_copy(zd, k):
        return rcopy(to_x.at[cut(zd, k), :], from_x.at[cut(zd, k), :], x_send.at[zd, k], x_recv.at[zd, k], x_peer)

    def z_copy(zd, way, k):
        step = 1 if way == 0 else -1
        return rcopy(
            to_z.at[cut(zd, k), :], from_z.at[way, cut(zd, k), :],
            z_send.at[way, zd, k], z_recv.at[way, zd, k], ((z + step) * 2 + x, vg),
        )

    def z_arrives(way):
        return z >= 1 if way == 0 else z + 1 < n_z

    order = [(d, way) for d in range(n_z - 1, 0, -1) for way in (0, 1)]

    def place(d, way):
        zd = z + d if way == 0 else z - d
        return zd, (zd >= 0) & (zd < n_z)

    def send_x(zd):
        for k in chunks:
            to_x[cut(zd, k), :] = part(last_b, zd * 2 + 1 - x, k).astype(BF16)
            x_copy(zd, k).start()

    for d, way in order:
        zd, there = place(d, way)
        pl.when(there)(lambda zd=zd: send_x(zd))
    send_x(z)
    small.second()

    for d, way in order:
        zd, there = place(d, way)

        @pl.when(there)
        def _(zd=zd, way=way):
            for k in chunks:
                x_copy(zd, k).wait_recv()
                value = part(last_b, zd * 2 + x, k) + from_x[cut(zd, k), :].astype(F32)

                @pl.when(z_arrives(way))
                def _(k=k, value=value):
                    z_copy(zd, way, k).wait_recv()
                    to_z[cut(zd, k), :] = (value + from_z[way, cut(zd, k), :].astype(F32)).astype(BF16)

                @pl.when(jnp.logical_not(z_arrives(way)))
                def _(k=k, value=value):
                    to_z[cut(zd, k), :] = value.astype(BF16)

                z_copy(zd, way, k).start()

    small.third()
    for k in chunks:
        x_copy(z, k).wait_recv()
        pre[here(k), :] = part(last_b, cg, k) + from_x[cut(z, k), :].astype(F32)
        for way in (0, 1):
            @pl.when(z_arrives(way))
            def _(way=way, k=k):
                z_copy(z, way, k).wait_recv()
                pre[here(k), :] += from_z[way, cut(z, k), :].astype(F32)

        lin = pre[here(k), :] * coef[here(k), :]
        pre[here(k), :] = lin
        term = dot(var_ref[here(k), :], lin, ((0,), (0,)))
        local_msg[...] = term if k == 0 else local_msg[...] + term
    big = Total(n_cg, n_vg, local_msg, grad_msg_ref, cuts_b, quarters_b, sem_b)
    big.start()
    grad_var_ref[...] = dot(pre[...], msg_w_ref[...], ((1,), (1,)))
    big.second()

    for k in chunks:
        for zs in range(n_z):
            gx_copy(zs, k).wait_send()
            x_copy(zs, k).wait_send()
        for d in range(n_z):
            for way in (0, 1):
                zs = z - d if way == 0 else z + d
                on(zs, way, lambda zs=zs, way=way, k=k: gz_copy(zs, way, k).wait_send())
        for d, way in order:
            zd, there = place(d, way)
            pl.when(there)(lambda zd=zd, way=way, k=k: z_copy(zd, way, k).wait_send())
        for h in range(n_hi):
            pass_copy(h, k).wait_send()
            core_copy(h, k).wait_send()
        for j in range(1, n_hi):
            peer_copy(j, k).wait_send()
            own_copy(j, k).wait_send()
    small.finish()
    big.third()
    big.finish()


def chains_kernel(row_blocks, row_ref, col_ref, out_ref):
    count = row_ref.shape[0]
    base = 0
    for index_ref, blocks in ((row_ref, row_blocks), (col_ref, out_ref.shape[0] - 2 * count - row_blocks)):
        last = base + count

        def clear(b, carry):
            out_ref[last + b] = count
            return carry

        lax.fori_loop(0, blocks, clear, 0)
        for k in range(count):
            at = last + index_ref[k]
            out_ref[base + k] = out_ref[at]
            out_ref[at] = k
        base = last + blocks


def chains(row_index, col_index, row_blocks, col_blocks):
    smem = pl.BlockSpec(memory_space=pltpu.SMEM)
    return pl.pallas_call(
        functools.partial(chains_kernel, row_blocks),
        name="chains",
        out_shape=jax.ShapeDtypeStruct((2 * row_index.shape[0] + row_blocks + col_blocks,), jnp.int32),
        in_specs=[smem] * 2,
        out_specs=smem,
    )(row_index, col_index)


def layer(row_index, col_index, patterns, var_embed, msg_weight, col_coef, con_embed, cotangent,
          self_weight, row_coef, time_embed, n_cg, n_vg):
    size = var_embed.shape[0]
    count = patterns.shape[0]
    n_z, n_hi, n_max = n_cg // 2, n_vg // 2, max(n_cg, n_vg)
    others = max(n_hi - 1, 1)
    row_blocks, col_blocks = n_vg * size // TB, n_cg * size // TB
    share = H // n_vg
    vmem, smem, anywhere = (pl.BlockSpec(memory_space=m) for m in (pltpu.VMEM, pltpu.SMEM, pl.ANY))
    full, square = jax.ShapeDtypeStruct((size, H), F32), jax.ShapeDtypeStruct((H, H), F32)
    dma = lambda *n: pltpu.SemaphoreType.DMA(n)
    return pl.pallas_call(
        functools.partial(layer_kernel, n_cg, n_vg),
        name="layer",
        out_shape=(full, full, full, square, square),
        in_specs=[smem, smem, smem, anywhere, vmem, vmem, vmem, anywhere, anywhere, vmem, vmem, vmem],
        out_specs=(vmem,) * 5,
        scratch_shapes=[
            pltpu.VMEM(patterns.shape, BF16),
            pltpu.VMEM((size, H), F32),
            pltpu.VMEM((size, H), F32),
            pltpu.VMEM((size, H), F32),
            pltpu.VMEM((size, H), F32),
            pltpu.VMEM((col_blocks, TB, H), BF16),
            pltpu.VMEM((row_blocks, TB, H), BF16),
            pltpu.VMEM((count + 1, TB, H), F32),
            pltpu.VMEM((n_hi * size, H), BF16),
            pltpu.VMEM((n_hi * size, H), BF16),
            pltpu.VMEM((others * size, H), BF16),
            pltpu.VMEM((others * size, H), BF16),
            pltpu.VMEM((n_z * size, H), BF16),
            pltpu.VMEM((n_z * size, H), BF16),
            pltpu.VMEM((n_z * size, H), BF16),
            pltpu.VMEM((2, n_z * size, H), BF16),
            pltpu.VMEM((H, H), F32),
            pltpu.VMEM((H, H), F32),
            pltpu.VMEM((n_vg - 1, share, H), F32),
            pltpu.VMEM((n_vg - 1, share, H), F32),
            pltpu.VMEM((n_cg, share, H), F32),
            pltpu.VMEM((n_cg, share, H), F32),
            dma(3), dma(2, n_z, CHUNKS), dma(n_z, CHUNKS), dma(n_z, CHUNKS), dma(n_z, CHUNKS),
            dma(n_hi, CHUNKS), dma(n_hi, CHUNKS), dma(others, CHUNKS), dma(others, CHUNKS),
            dma(others, CHUNKS), dma(n_hi, CHUNKS), dma(others, CHUNKS), dma(n_hi, CHUNKS),
            dma(n_z, CHUNKS), dma(n_z, CHUNKS), dma(2, n_z, CHUNKS), dma(2, n_z, CHUNKS),
            dma(6, n_max), dma(6, n_max),
        ],
        compiler_params=pltpu.CompilerParams(
            collective_id=0, has_side_effects=True, vmem_limit_bytes=60000 * 1024
        ),
    )(
        row_index, col_index, chains(row_index, col_index, row_blocks, col_blocks), patterns, var_embed, msg_weight, col_coef.reshape(-1, H),
        con_embed, cotangent, self_weight, row_coef.reshape(-1, H), time_embed.reshape(1, H),
    )


def finish_kernel(*refs):
    half = len(refs) // 2
    for source, target in zip(refs[:half], refs[half:]):
        target[...] = source[...]


def finish(*arrays):
    steps = 2
    specs = [pl.BlockSpec((a.shape[0] // steps, H), lambda i: (i, 0)) for a in arrays]
    return pl.pallas_call(
        finish_kernel,
        name="finish",
        grid=(steps,),
        out_shape=tuple(jax.ShapeDtypeStruct(a.shape, a.dtype) for a in arrays),
        in_specs=specs,
        out_specs=tuple(specs),
    )(*arrays)


def body(
    con_embed, var_embed, row_coef, col_coef, self_weight, msg_weight,
    timestep, tile_rows, tile_cols, pattern, cotangent,
):
    n_cg, n_vg = lax.axis_size("cg"), lax.axis_size("vg")
    frequency = jnp.exp(-math.log(10000.0) * jnp.arange(H // 2, dtype=F32) / (H // 2))
    phases = timestep[0].astype(F32) * frequency
    time_embed = jnp.concatenate([jnp.sin(phases), jnp.cos(phases)])
    return finish(*layer(
        tile_rows.reshape(-1), tile_cols.reshape(-1), pattern.reshape(-1, TB, TB), var_embed, msg_weight,
        col_coef, con_embed, cotangent, self_weight, row_coef, time_embed, n_cg, n_vg,
    ))


def solution(mesh):
    in_specs = (
        P(("cg", "vg"), None),
        P(("vg", "cg"), None),
        P(("cg", "vg")),
        P(("vg", "cg")),
        P(),
        P(),
        P(),
        P("cg", "vg", None),
        P("cg", "vg", None),
        P("cg", "vg", None, None, None),
        P(("cg", "vg"), None),
    )
    out_specs = (P(("cg", "vg"), None), P(("cg", "vg"), None), P(("vg", "cg"), None), P(), P())
    return jax.shard_map(body, mesh=mesh, in_specs=in_specs, out_specs=out_specs, check_vma=False)
```

profile of v0, /device:TPU:0, one launch (start us, length us, event | category | flops | bytes accessed | tf_op | source)
XLA Modules:
  0.0 98.6 jit_solution(3978648125651351926)
XLA Ops:
  1.3 1.5 %chains.1.chain_ref = s32[56]{0:T(128)} custom-call(s32[16]{0:T(128)} %bitcast.11, s32[16]{0:T(128)} %bitcast.13), custom_call_target="tpu_custom_call" | custom-call | tf_op jit(solution)/shard_map/chains/pallas_call | solution.py:398
  2.8 0.1 fusion
  2.8 0.6 maximum_bitcast_fusion.time_ref
  3.4 92.8 %layer.1 = (f32[1024,128]{1,0:T(8,128)}, f32[1024,128]{1,0:T(8,128)}, f32[1024,128]{1,0:T(8,128)}, f32[128,128]{1,0:T(8,128)}, f32[128,128]{1,0:T(8,128)}) custom-call(s32[16]{0:T(128)} %bitcast.12, s32[16]{0:T(128)} %bitcast.14, s32[56]{0:T(128)} %chains.1.chain_ref, bf16[16,512,512]{2,1,0:T(8,128)(2,1)} %bitcast.8, f32[1024,128]{1,0:T(8,128)} %var_ref.1, ...), custom_call_target="tpu_custom_call" | custom-call | tf_op jit(solution)/shard_map/layer/pallas_call | solution.py:418
  96.2 2.4 %finish.1 = (f32[1024,128]{1,0:T(8,128)}, f32[1024,128]{1,0:T(8,128)}, f32[1024,128]{1,0:T(8,128)}, f32[128,128]{1,0:T(8,128)}, f32[128,128]{1,0:T(8,128)}) custom-call(f32[1024,128]{1,0:T(8,128)} %get-tuple-element.10.refs_0_, f32[1024,128]{1,0:T(8,128)} %get-tuple-element.11.refs_1_, f32[1024,128]{1,0:T(8,128)} %get-tuple-element.12.refs_2_, ...), custom_call_target="tpu_custom_call" | custom-call | tf_op jit(solution)/shard_map/finish/pallas_call | solution.py:471
where the time goes:
time: 98.7 us; the launch traced here: 98.6 us
  Pallas kernels  96.6 us (98%)
  between operations  1.3 us (1%)
    pallas_call x1, Pallas kernels, layer(): pl.pallas_call(functools.partial(layer_kernel, n_cg, n_vg), name='layer',...  92.8 us
    pallas_call x1, Pallas kernels, finish(): pl.pallas_call(finish_kernel, name='finish', grid=(steps,), out_shape=tup...  2.38 us

commit v1 on v0

v1 whole, which is shorter than its diff:
```python
import functools
import math

import jax
import jax.numpy as jnp
import numpy as np
from jax import lax
from jax.experimental import pallas as pl
from jax.experimental.pallas import tpu as pltpu
from jax.sharding import PartitionSpec as P

H = 128
TB = 512
CHUNKS = 4
MESH = pl.DeviceIdType.MESH
HIGHEST = lax.Precision.HIGHEST
F32 = jnp.float32
BF16 = jnp.bfloat16


def rcopy(src, dst, send_sem, recv_sem, device):
    return pltpu.make_async_remote_copy(
        src_ref=src, dst_ref=dst, send_sem=send_sem, recv_sem=recv_sem,
        device_id=device, device_id_type=MESH,
    )


def rows(index, size):
    return pl.ds(pl.multiple_of(index * size, size), size)


def dot(a, b, dims=((1,), (0,))):
    return lax.dot_general(a, b, (dims, ((), ())), precision=HIGHEST, preferred_element_type=F32)


def column(coef_ref, out_ref):
    for i in range(coef_ref.shape[0]):
        out_ref[pl.ds(i * H, H), :] = jnp.broadcast_to(coef_ref[pl.ds(i, 1), :], (H, H)).T


class Total:
    def __init__(self, n_cg, n_vg, local, out, cuts, parts, sem):
        self.n_cg, self.n_vg = n_cg, n_vg
        self.local, self.out, self.cuts, self.parts, self.sem = local, out, cuts, parts, sem
        self.cg, self.vg = lax.axis_index("cg"), lax.axis_index("vg")
        self.size = H // n_cg

    def a(self, j):
        c = lax.rem(self.cg + j, self.n_cg)
        return rcopy(
            self.local.at[:, rows(c, self.size), :], self.cuts.at[j - 1],
            self.sem.at[0, j], self.sem.at[1, j], (c, self.vg),
        )

    def b(self, j):
        v = lax.rem(self.vg + j, self.n_vg)
        block = self.parts.at[self.vg]
        return rcopy(block, block, self.sem.at[2, j], self.sem.at[3, j], (self.cg, v))

    def b_wait(self, j):
        v = lax.rem(self.vg + self.n_vg - j, self.n_vg)
        block = self.parts.at[v]
        rcopy(block, block, self.sem.at[2, j], self.sem.at[3, j], (self.cg, v)).wait_recv()

    def c(self, j):
        c = lax.rem(self.cg + j, self.n_cg)
        block = self.out.at[:, rows(self.cg, self.size), :]
        return rcopy(block, block, self.sem.at[4, j], self.sem.at[5, j], (c, self.vg))

    def c_wait(self, j):
        c = lax.rem(self.cg + self.n_cg - j, self.n_cg)
        block = self.out.at[:, rows(c, self.size), :]
        rcopy(block, block, self.sem.at[4, j], self.sem.at[5, j], (c, self.vg)).wait_recv()

    def start(self):
        for j in range(1, self.n_cg):
            self.a(j).start()

    def second(self):
        value = self.local[:, rows(self.cg, self.size), :]
        for j in range(1, self.n_cg):
            self.a(j).wait_recv()
            value = value + self.cuts[j - 1]
        self.parts[self.vg] = value
        for j in range(1, self.n_vg):
            self.b(j).start()

    def third(self):
        for j in range(1, self.n_vg):
            self.b_wait(j)
        value = self.parts[0]
        for v in range(1, self.n_vg):
            value = value + self.parts[v]
        self.out[:, rows(self.cg, self.size), :] = value
        for j in range(1, self.n_cg):
            self.c(j).start()

    def finish(self):
        for j in range(1, self.n_cg):
            self.c_wait(j)
            self.c(j).wait_send()
            self.a(j).wait_send()
        for j in range(1, self.n_vg):
            self.b(j).wait_send()


def chains(count, row_blocks, col_blocks, row_ref, col_ref, out_ref):
    base = 0
    for index_ref, blocks in ((row_ref, row_blocks), (col_ref, col_blocks)):
        index = [index_ref[k] for k in range(count)]
        for k in range(count):
            at = jnp.int32(count)
            for j in range(k):
                at = jnp.where(index[j] == index[k], j, at)
            out_ref[base + k] = at

        def last(b, carry):
            at = jnp.int32(count)
            for k in range(count):
                at = jnp.where(index[k] == b, k, at)
            out_ref[base + count + b] = at
            return carry

        lax.fori_loop(0, blocks, last, 0)
        base = base + count + blocks


def layer_kernel(
    n_cg, n_vg, row_ref, col_ref, step_ref, pattern_hbm, var_ref, msg_w_ref, col_coef_ref, con_hbm, cot_hbm,
    self_w_ref, row_coef_ref, freq_ref,
    update_ref, grad_con_ref, grad_var_ref, grad_msg_ref, grad_self_ref,
    pattern, con_ref, cot_ref, col_scale, row_scale, pre, sums, grads, projected_a, projected_b, whole_a, whole_b, acc, chain_ref,
    to_core, from_core, to_peer, from_peer, to_x, from_x, to_z, from_z, to_q, from_q,
    local, total, cuts, parts,
    load_sem, gz_send, gx_send, gz_recv, gx_recv, gq_send, gq_recv,
    core_send, core_recv, peer_send, peer_recv, own_send, pass_send, block_recv, pair_recv,
    x_send, x_recv, z_send, z_recv, q_send, q_recv, total_sem,
):
    n_z, n_hi = n_cg // 2, n_vg // 2
    cg, vg = lax.axis_index("cg"), lax.axis_index("vg")
    z, x = cg // 2, cg % 2
    hi, core = vg // 2, vg % 2
    count = pattern.shape[0]
    size = var_ref.shape[0]
    piece = size // CHUNKS
    tiles = size // TB
    halves = CHUNKS // tiles
    half = TB // halves
    chunks = range(CHUNKS)
    early, late = range(tiles), range(CHUNKS - tiles, CHUNKS)
    projected, whole = (projected_a, projected_b), (whole_a, whole_b)
    odd = z % 2
    mate = z + 1 - 2 * odd
    x_peer, z_mate, pair = (z * 2 + 1 - x, vg), (mate * 2 + x, vg), (cg, hi * 2 + 1 - core)

    barrier = pltpu.get_barrier_semaphore()
    for j in range(1, n_cg):
        pl.semaphore_signal(barrier, inc=1, device_id=(lax.rem(cg + j, n_cg), vg), device_id_type=MESH)
    for j in range(1, n_vg):
        pl.semaphore_signal(barrier, inc=1, device_id=(cg, lax.rem(vg + j, n_vg)), device_id_type=MESH)
    loads = [
        pltpu.make_async_copy(con_hbm, con_ref, load_sem.at[0]),
        pltpu.make_async_copy(cot_hbm, cot_ref, load_sem.at[1]),
        pltpu.make_async_copy(pattern_hbm, pattern, load_sem.at[2]),
    ]
    for load in loads:
        load.start()

    def of(h):
        return range(h * tiles, (h + 1) * tiles)

    def cut(block, k):
        return rows(block * CHUNKS + k, piece)

    def here(k):
        return pl.ds((k % tiles) * TB + (k // tiles) * half, half)

    def inner(k):
        return pl.ds((k // tiles) * half, half)

    def spot(parts_of, block, k):
        return parts_of[k // tiles].at[block * tiles + k % tiles]

    def gz_copy(zs, way, k):
        block = spot(projected, zs * 2 + x, k)
        step = 1 if way == 0 else -1
        return rcopy(block, block, gz_send.at[way, zs, k], gz_recv.at[zs, k], ((z + step) * 2 + x, vg))

    def gx_copy(zs, k):
        block = spot(projected, zs * 2 + x, k)
        return rcopy(block, block, gx_send.at[zs, k], gx_recv.at[zs, k], x_peer)

    def gx_wait(zs, k):
        block = spot(projected, zs * 2 + 1 - x, k)
        rcopy(block, block, gx_send.at[zs, k], gx_recv.at[zs, k], x_peer).wait_recv()

    def gq_copy(k):
        block = spot(projected, z * 2 + 1 - x, k)
        return rcopy(block, block, gq_send.at[k - late[0]], gq_recv.at[k - late[0]], z_mate)

    def gq_wait(k):
        block = spot(projected, mate * 2 + 1 - x, k)
        rcopy(block, block, gq_send.at[k - late[0]], gq_recv.at[k - late[0]], z_mate).wait_recv()

    def on(zs, way, act):
        if way == 0:
            pl.when((zs >= 0) & (zs <= z) & (z + 1 < n_z))(act)
        else:
            pl.when((zs < n_z) & (zs >= z) & (z >= 1))(act)

    def by_x(d, way, k):
        if d != 1 or k not in late:
            return None
        return odd == 0 if way == 0 else odd == 1

    def by_x_back(zd, k):
        return zd != mate if k in early else None

    def when(condition, act):
        if condition is None:
            act()
        else:
            pl.when(condition)(act)

    column(col_coef_ref, col_scale)
    for k in chunks:
        spot(projected, cg, k)[...] = (var_ref[here(k), :] * col_scale[here(k), :]).astype(BF16)
        if k == 0:
            pl.semaphore_wait(barrier, n_cg + n_vg - 2)
        for way in (0, 1):
            on(z, way, lambda way=way: gz_copy(z, way, k).start())
        gx_copy(z, k).start()

    acc[count] = jnp.zeros(acc.shape[1:], F32)
    row_blocks = whole_a.shape[0]
    chains(count, row_blocks, projected_a.shape[0], row_ref, col_ref, chain_ref)
    last_f, prev_b, last_b = count, count + row_blocks, 2 * count + row_blocks

    for d in range(1, n_z):
        for k in chunks:
            for way in (0, 1):
                zs = z - d if way == 0 else z + d

                @pl.when((zs >= 0) & (zs < n_z))
                def _(zs=zs, way=way, k=k, d=d):
                    gz_copy(zs, way, k).wait_recv()
                    on(zs, way, lambda: gz_copy(zs, way, k).start())
                    when(by_x(d, way, k), lambda: gx_copy(zs, k).start())

        to_go = n_z - 1 - z
        if d == 1:
            turn = ((odd == 0) & (z <= 1)) | ((odd == 1) & (to_go <= 1))
        else:
            turn = ((odd == 0) & (z == d)) | ((odd == 1) & (to_go == d))

        @pl.when(turn)
        def _():
            for k in late:
                gx_wait(z, k)
                gq_copy(k).start()

    for load in loads[:2]:
        load.wait()
    phases = step_ref[0].astype(F32) * freq_ref[...]
    lane = lax.broadcasted_iota(jnp.int32, phases.shape, 1)
    time_embed = jnp.where(lane < H // 2, jnp.sin(phases), jnp.cos(phases))
    pre[...] = dot(con_ref[...], self_w_ref[...]) + time_embed
    column(row_coef_ref, row_scale)
    loads[2].wait()

    def tile_first(from_ref, source_refs, side):
        def step(k, carry):
            source = source_refs[0][from_ref[k]]
            tile = pattern[k, :, pl.ds(0, half)] if side == 1 else pattern[k, pl.ds(0, half), :]
            acc[k] = lax.dot_general(tile, source, (((side,), (0,)), ((), ())), preferred_element_type=F32)
            return carry

        lax.fori_loop(0, count, step, 0, unroll=4)

    def tile_next(prev, from_ref, source_refs, side, h, m):
        deep, span = pl.ds(h * half, half), pl.ds(m * half, half)

        def step(k, carry):
            source = source_refs[h][from_ref[k]]
            tile = pattern[k, span, deep] if side == 1 else pattern[k, deep, span]
            product = lax.dot_general(tile, source, (((side,), (0,)), ((), ())), preferred_element_type=F32)
            value = acc[k, span, :] + product
            if h == halves - 1:
                value = value + acc[chain_ref[prev + k], span, :]
            acc[k, span, :] = value
            return carry

        lax.fori_loop(0, count, step, 0, unroll=4)

    def part(last, block, k):
        tile = chain_ref[last + block * tiles + k % tiles]
        return acc[tile, inner(k), :]

    base = z - odd
    for h in range(halves):
        for k in of(h):
            if k in late:
                gq_wait(k)
                for j in range(2, n_z):
                    gx_wait(lax.rem(base + j, n_z), k)
            else:
                for zs in range(n_z):
                    gx_wait(zs, k)
        if h == 0:
            tile_first(col_ref, projected, 1)
        elif h < halves - 1:
            for m in range(halves):
                tile_next(0, col_ref, projected, 1, h, m)

    ups = [lax.rem(hi + j, n_hi) for j in range(n_hi)]
    downs = [lax.rem(hi + n_hi - j, n_hi) for j in range(n_hi)]

    def core_copy(h, k):
        return rcopy(
            to_core.at[cut(h, k), :], from_core.at[cut(h, k), :], core_send.at[h, k], core_recv.at[h, k], pair
        )

    def peer_copy(j, k):
        return rcopy(
            to_peer.at[cut(j - 1, k), :], from_peer.at[cut(j - 1, k), :],
            peer_send.at[j - 1, k], peer_recv.at[j - 1, k], (cg, ups[j] * 2 + core),
        )

    def own_copy(j, k):
        block = spot(whole, vg, k)
        return rcopy(block, block, own_send.at[j - 1, k], block_recv.at[j - 1, k], (cg, ups[j] * 2 + core))

    def block_wait(j, k):
        block = spot(whole, downs[j] * 2 + core, k)
        rcopy(block, block, own_send.at[j - 1, k], block_recv.at[j - 1, k], pair).wait_recv()

    def pass_copy(h, k):
        block = spot(whole, h * 2 + core, k)
        return rcopy(block, block, pass_send.at[h, k], pair_recv.at[h, k], pair)

    def pass_wait(h, k):
        block = spot(whole, h * 2 + 1 - core, k)
        rcopy(block, block, pass_send.at[h, k], pair_recv.at[h, k], pair).wait_recv()

    for m in range(halves):
        tile_next(0, col_ref, projected, 1, halves - 1, m)
        for j in list(range(1, n_hi)) + [0]:
            for k in of(m):
                to_core[cut(ups[j], k), :] = part(last_f, ups[j] * 2 + 1 - core, k).astype(BF16)
                core_copy(ups[j], k).start()
    for j in range(1, n_hi):
        for k in chunks:
            core_copy(ups[j], k).wait_recv()
            to_peer[cut(j - 1, k), :] = (
                part(last_f, ups[j] * 2 + core, k) + from_core[cut(ups[j], k), :].astype(F32)
            ).astype(BF16)
            peer_copy(j, k).start()
    for k in chunks:
        core_copy(hi, k).wait_recv()
        value = part(last_f, vg, k) + from_core[cut(hi, k), :].astype(F32)
        for j in range(1, n_hi):
            peer_copy(j, k).wait_recv()
            value = value + from_peer[cut(j - 1, k), :].astype(F32)
        sums[here(k), :] = value
        preact = pre[here(k), :] + row_scale[here(k), :] * dot(value, msg_w_ref[...])
        sig = jax.nn.sigmoid(preact)
        grad_pre = cot_ref[here(k), :] * sig * (1.0 + preact * (1.0 - sig))
        grad = row_scale[here(k), :] * grad_pre
        spot(whole, vg, k)[...] = dot(grad, msg_w_ref[...], ((1,), (1,))).astype(BF16)
        for j in range(1, n_hi):
            own_copy(j, k).start()
        pass_copy(hi, k).start()
        grads[here(k), :] = grad
        update_ref[here(k), :] = con_ref[here(k), :] + preact * sig
        pre[here(k), :] = grad_pre
    small = Total(n_cg, n_vg, local, total, cuts, parts, total_sem)

    def take(h):
        for k in of(h):
            for j in range(1, n_hi):
                block_wait(j, k)
                pass_copy(downs[j], k).start()

    take(0)
    local[0] = dot(sums[...], grads[...], ((0,), (0,)))
    local[1] = dot(con_ref[...], pre[...], ((0,), (0,)))
    small.start()
    for h in range(halves):
        if h > 0:
            take(h)
        for k in of(h):
            for hb in range(n_hi):
                pass_wait(hb, k)
        if h == 0:
            tile_first(row_ref, whole, 0)
        elif h < halves - 1:
            for m in range(halves):
                tile_next(prev_b, row_ref, whole, 0, h, m)

    def x_copy(zd, k):
        return rcopy(to_x.at[cut(zd, k), :], from_x.at[cut(zd, k), :], x_send.at[zd, k], x_recv.at[zd, k], x_peer)

    def q_copy(k):
        return rcopy(to_q.at[rows(k, piece), :], from_q.at[rows(k, piece), :], q_send.at[k], q_recv.at[k], z_mate)

    def z_copy(zd, way, k):
        step = 1 if way == 0 else -1
        return rcopy(
            to_z.at[cut(zd, k), :], from_z.at[way, cut(zd, k), :],
            z_send.at[way, zd, k], z_recv.at[way, zd, k], ((z + step) * 2 + x, vg),
        )

    def z_arrives(way):
        return z >= 1 if way == 0 else z + 1 < n_z

    turns = range(n_z - 1)

    def targets(t):
        yield n_z - 1 - t, 0, n_z - 1 - t > z
        yield t, 1, t < z

    def send_x(zd, k):
        to_x[cut(zd, k), :] = part(last_b, zd * 2 + 1 - x, k).astype(BF16)
        x_copy(zd, k).start()

    def send_turn(t, span):
        for zd, way, there in targets(t):

            @pl.when(there)
            def _(zd=zd):
                for k in span:
                    when(by_x_back(zd, k), lambda: send_x(zd, k))

    for m in range(halves):
        tile_next(prev_b, row_ref, whole, 0, halves - 1, m)
        for k in of(m):
            if k in early:
                to_q[rows(k, piece), :] = part(last_b, mate * 2 + 1 - x, k).astype(BF16)
                q_copy(k).start()
        send_turn(0, of(m))
    for t in turns[1:]:
        send_turn(t, chunks)
    grad_con_ref[...] = cot_ref[...] + dot(pre[...], self_w_ref[...], ((1,), (1,)))

    for t in turns:
        for k in chunks:
            for zd, way, there in targets(t):

                @pl.when(there)
                def _(zd=zd, way=way, k=k):
                    sums[here(k), :] = part(last_b, zd * 2 + x, k)

                    def from_peer_x():
                        x_copy(zd, k).wait_recv()
                        sums[here(k), :] += from_x[cut(zd, k), :].astype(F32)

                    when(by_x_back(zd, k), from_peer_x)

                    @pl.when(z_arrives(way))
                    def _():
                        z_copy(zd, way, k).wait_recv()
                        sums[here(k), :] += from_z[way, cut(zd, k), :].astype(F32)

                    to_z[cut(zd, k), :] = sums[here(k), :].astype(BF16)
                    z_copy(zd, way, k).start()

            if t == 0 and k == 1:
                small.second()
        if t == 0:
            small.third()
            for k in chunks:
                if k in early:
                    q_copy(k).wait_recv()
                    to_x[cut(z, k), :] = (
                        part(last_b, z * 2 + 1 - x, k) + from_q[rows(k, piece), :].astype(F32)
                    ).astype(BF16)
                    x_copy(z, k).start()
                else:
                    send_x(z, k)

    for k in chunks:
        x_copy(z, k).wait_recv()
        sums[here(k), :] = part(last_b, cg, k) + from_x[cut(z, k), :].astype(F32)
        for way in (0, 1):
            @pl.when(z_arrives(way))
            def _(way=way, k=k):
                z_copy(z, way, k).wait_recv()
                sums[here(k), :] += from_z[way, cut(z, k), :].astype(F32)

        grad_var_ref[here(k), :] = sums[here(k), :] * col_scale[here(k), :]

    small.finish()
    grad_msg_ref[...] = total[0]
    grad_self_ref[...] = total[1]
    for k in chunks:
        for d in range(n_z):
            for way in (0, 1) if d else (0,):
                zs = z - d if way == 0 else z + d

                @pl.when((zs >= 0) & (zs < n_z))
                def _(zs=zs, d=d, way=way, k=k):
                    when(by_x(d, way, k), lambda: gx_copy(zs, k).wait_send())

        x_copy(z, k).wait_send()
        for d in range(n_z):
            for way in (0, 1):
                zs = z - d if way == 0 else z + d
                on(zs, way, lambda zs=zs, way=way, k=k: gz_copy(zs, way, k).wait_send())
        for t in turns:
            for zd, way, there in targets(t):

                @pl.when(there)
                def _(zd=zd, way=way, k=k):
                    when(by_x_back(zd, k), lambda: x_copy(zd, k).wait_send())
                    z_copy(zd, way, k).wait_send()

        for h in range(n_hi):
            pass_copy(h, k).wait_send()
            core_copy(h, k).wait_send()
        for j in range(1, n_hi):
            peer_copy(j, k).wait_send()
            own_copy(j, k).wait_send()
        if k in late:
            gq_copy(k).wait_send()
        if k in early:
            q_copy(k).wait_send()


def layer(row_index, col_index, timestep, patterns, var_embed, msg_weight, col_coef, con_embed, cotangent,
          self_weight, row_coef, frequency, n_cg, n_vg):
    size = var_embed.shape[0]
    count = patterns.shape[0]
    n_z, n_hi, n_max = n_cg // 2, n_vg // 2, max(n_cg, n_vg)
    others = max(n_hi - 1, 1)
    row_blocks, col_blocks = n_vg * size // TB, n_cg * size // TB
    early = size // TB
    share = H // n_cg
    vmem, smem, anywhere = (pl.BlockSpec(memory_space=m) for m in (pltpu.VMEM, pltpu.SMEM, pl.ANY))
    full, square = pltpu.VMEM((size, H), F32), pltpu.VMEM((H, H), F32)
    dma = lambda *n: pltpu.SemaphoreType.DMA(n)
    return pl.pallas_call(
        functools.partial(layer_kernel, n_cg, n_vg),
        name="layer",
        out_shape=(full, full, full, square, square),
        in_specs=[smem, smem, smem, anywhere, vmem, vmem, vmem, anywhere, anywhere, vmem, vmem, vmem],
        out_specs=(vmem,) * 5,
        scratch_shapes=[
            pltpu.VMEM(patterns.shape, BF16),
            *[pltpu.VMEM((size, H), F32)] * 7,
            *[pltpu.VMEM((col_blocks, TB // 2, H), BF16)] * 2,
            *[pltpu.VMEM((row_blocks, TB // 2, H), BF16)] * 2,
            pltpu.VMEM((count + 1, TB, H), F32),
            pltpu.SMEM((2 * count + row_blocks + col_blocks,), jnp.int32),
            pltpu.VMEM((n_hi * size, H), BF16),
            pltpu.VMEM((n_hi * size, H), BF16),
            pltpu.VMEM((others * size, H), BF16),
            pltpu.VMEM((others * size, H), BF16),
            pltpu.VMEM((n_z * size, H), BF16),
            pltpu.VMEM((n_z * size, H), BF16),
            pltpu.VMEM((n_z * size, H), BF16),
            pltpu.VMEM((2, n_z * size, H), BF16),
            pltpu.VMEM((early * (size // CHUNKS), H), BF16),
            pltpu.VMEM((early * (size // CHUNKS), H), BF16),
            pltpu.VMEM((2, H, H), F32),
            pltpu.VMEM((2, H, H), F32),
            pltpu.VMEM((n_cg - 1, 2, share, H), F32),
            pltpu.VMEM((n_vg, 2, share, H), F32),
            dma(3), dma(2, n_z, CHUNKS), dma(n_z, CHUNKS), dma(n_z, CHUNKS), dma(n_z, CHUNKS),
            dma(early), dma(early),
            dma(n_hi, CHUNKS), dma(n_hi, CHUNKS), dma(others, CHUNKS), dma(others, CHUNKS),
            dma(others, CHUNKS), dma(n_hi, CHUNKS), dma(others, CHUNKS), dma(n_hi, CHUNKS),
            dma(n_z, CHUNKS), dma(n_z, CHUNKS), dma(2, n_z, CHUNKS), dma(2, n_z, CHUNKS),
            dma(early), dma(early), dma(6, n_max),
        ],
        compiler_params=pltpu.CompilerParams(
            collective_id=0, has_side_effects=True, vmem_limit_bytes=60000 * 1024
        ),
    )(
        row_index, col_index, timestep, patterns, var_embed, msg_weight, col_coef.reshape(-1, H),
        con_embed, cotangent, self_weight, row_coef.reshape(-1, H), frequency,
    )


def finish_kernel(*refs):
    count = (len(refs) - 1) // 2
    copies = [pltpu.make_async_copy(refs[i], refs[count + i], refs[-1].at[i]) for i in range(count)]
    for copy in copies:
        copy.start()
    for copy in copies:
        copy.wait()


def finish(*arrays):
    return pl.pallas_call(
        finish_kernel,
        name="finish",
        out_shape=tuple(jax.ShapeDtypeStruct(a.shape, a.dtype) for a in arrays),
        in_specs=[pl.BlockSpec(memory_space=pltpu.VMEM)] * len(arrays),
        out_specs=(pl.BlockSpec(memory_space=pl.ANY),) * len(arrays),
        scratch_shapes=[pltpu.SemaphoreType.DMA((len(arrays),))],
    )(*[pltpu.with_memory_space_constraint(a, pltpu.VMEM) for a in arrays])


def body(
    con_embed, var_embed, row_coef, col_coef, self_weight, msg_weight,
    timestep, tile_rows, tile_cols, pattern, cotangent,
):
    n_cg, n_vg = lax.axis_size("cg"), lax.axis_size("vg")
    frequency = np.exp(-math.log(10000.0) * np.arange(H // 2) / (H // 2))
    frequency = jnp.asarray(np.concatenate([frequency, frequency])[None, :], F32)
    return finish(*layer(
        tile_rows.reshape(-1), tile_cols.reshape(-1), timestep, pattern.reshape(-1, TB, TB), var_embed, msg_weight,
        col_coef, con_embed, cotangent, self_weight, row_coef, frequency, n_cg, n_vg,
    ))


def solution(mesh):
    in_specs = (
        P(("cg", "vg"), None),
        P(("vg", "cg"), None),
        P(("cg", "vg")),
        P(("vg", "cg")),
        P(),
        P(),
        P(),
        P("cg", "vg", None),
        P("cg", "vg", None),
        P("cg", "vg", None, None, None),
        P(("cg", "vg"), None),
    )
    out_specs = (P(("cg", "vg"), None), P(("cg", "vg"), None), P(("vg", "cg"), None), P(), P())
    return jax.shard_map(body, mesh=mesh, in_specs=in_specs, out_specs=out_specs, check_vma=False)
```

time: 98.7 us -> 92.9 us (0.941)
  Pallas kernels: 96.6 us -> 91.3 us
    pallas_call x1, Pallas kernels: 92.8 us -> 90.1 us  [layer(): pl.pallas_call(functools.partial(layer_kernel, n_cg, n_vg), name='layer',...]
    pallas_call x2 -> x1, Pallas kernels: 3.85 us -> 1.22 us  [finish(): pl.pallas_call(finish_kernel, name='finish', out_shape=tuple((jax.ShapeDt...]
where the time goes in v1:
time: 92.9 us; the launch traced here: 92.6 us
  Pallas kernels  91.3 us (98%)
  between operations  1.29 us (1%)
    pallas_call x1, Pallas kernels, layer(): pl.pallas_call(functools.partial(layer_kernel, n_cg, n_vg), name='layer',...  90.1 us

profile of v1, /device:TPU:0, one launch (start us, length us, event | category | flops | bytes accessed | tf_op | source)
XLA Modules:
  0.0 92.6 jit_solution(13589260765185526988)
XLA Ops:
  1.3 90.1 %layer.1 = (f32[1024,128]{1,0:T(8,128)S(1)}, f32[1024,128]{1,0:T(8,128)S(1)}, f32[1024,128]{1,0:T(8,128)S(1)}, f32[128,128]{1,0:T(8,128)S(1)}, f32[128,128]{1,0:T(8,128)S(1)}) custom-call(s32[16]{0:T(128)} %bitcast.8, s32[16]{0:T(128)} %bitcast.9, s32[1]{0:T(128)S(6)} %copy.17.step_ref, bf16[16,512,512]{2,1,0:T(8,128)(2,1)} %bitcast.5, f32[1024,128]{1,0:T(8,128)} %var_ref.1, ...), custom_call_target="tpu_custom_call" | custom-call | tf_op jit(solution)/shard_map/layer/pallas_call | solution.py:541
  91.4 1.2 %finish.1 = (f32[1024,128]{1,0:T(8,128)}, f32[1024,128]{1,0:T(8,128)}, f32[1024,128]{1,0:T(8,128)}, f32[128,128]{1,0:T(8,128)}, f32[128,128]{1,0:T(8,128)}) custom-call(f32[1024,128]{1,0:T(8,128)S(1)} %get-tuple-element.10.refs_0_, f32[1024,128]{1,0:T(8,128)S(1)} %get-tuple-element.11.refs_1_, f32[1024,128]{1,0:T(8,128)S(1)} %get-tuple-element.12.refs_2_, ...), custom_call_target="tpu_custom_call" | custom-call | tf_op jit(solution)/shard_map/finish/pallas_call | solution.py:594
